TPU v7x, 32 devices: a whole 2x2x4 slice. The times are simulated.
32 devices in a mesh: group: 4 (over y, core), owner: 8 (over z, x).
Axes of the slice: x: 2, y: 2, z: 4, core: 2. Of those that a mesh axis runs over, the one named last changes fastest.
Arguments:
- queries: bfloat16 [2048, 4096], P(('group', 'owner')), may hold values from -0.099609375 to 0.099609375
- passages: bfloat16 [2048, 4096], P(('group', 'owner')), may hold values from -0.099609375 to 0.099609375
- send_order: int32 [32, 64], P(('group', 'owner')), may hold values from 0 to 63, each once within a row
- neg_rows: int32 [32, 8], P(('group', 'owner')), may hold values from 0 to 63
Outputs:
- query_grad: bfloat16 [2048, 4096], P(('group', 'owner'))
- passage_grad: bfloat16 [2048, 4096], P(('group', 'owner'))
- row_loss: float32 [2048], P(('group', 'owner'))
Inputs may be any that keep to these rules, and one draw needn't show every extreme that they name: `send_order`: each row is a permutation of 0 .. 63. `neg_rows`: rows of the device's cluster, repeats allowed.
All inputs are finite; a program needn't handle non-finite values.
Results may differ from a plain program's by a relative error of at most 0.0053.
Values may be sent and summed in bfloat16 or wider, within the bound.
A program may use at most 64 MiB of HBM per device.

v0:
```python
import functools

import jax
import jax.numpy as jnp
from jax import lax
from jax.experimental import pallas as pl
from jax.experimental.pallas import tpu as pltpu
from jax.sharding import PartitionSpec as P

logit_scale = 1.0 / 0.05
epsilon = 1e-06
MESH = pl.DeviceIdType.MESH
f32, bf16 = jnp.float32, jnp.bfloat16


def xor(a, b, size):
    out, bit = 0, 1
    while bit < size:
        out = out + ((a // bit + b // bit) % 2) * bit
        bit *= 2
    return out


def dot(a, b, dims=((1,), (0,))):
    return lax.dot_general(a, b, (dims, ((), ())), preferred_element_type=f32)


def kernel(
    owners, groups, step_peers,
    q_ref, p_ref, send_col, send_row, neg_col, neg_row,
    q_out, p_out, loss_out,
    sent, owned, keys, qh, coef, dp, negs, term, term_in, stage, back,
    send_sem, recv_sem, gsend_sem, grecv_sem,
):
    rows, width = q_ref.shape
    c = rows // owners
    n_neg = neg_col.shape[0]
    n_all = groups * n_neg
    steps = owners // step_peers
    span = step_peers * c
    g, o = lax.axis_index("group"), lax.axis_index("owner")
    my_step = o // step_peers

    barrier = pltpu.get_barrier_semaphore()

    @pl.loop(1, owners)
    def _(k):
        pl.semaphore_signal(barrier, inc=1, device_id=(g, xor(o, k, owners)), device_id_type=MESH)

    @pl.loop(1, groups)
    def _(k):
        pl.semaphore_signal(barrier, inc=1, device_id=(xor(g, k, groups), o), device_id_type=MESH)

    pick = (send_col[...] == lax.broadcasted_iota(jnp.int32, (rows, rows), 1)).astype(f32).astype(bf16)
    sent[0] = dot(pick, p_ref[...]).reshape(owners, c, width).astype(bf16)
    sent[1] = dot(pick, q_ref[...]).reshape(owners, c, width).astype(bf16)
    pl.semaphore_wait(barrier, owners + groups - 2)

    def copy_in(kind, src_slot, dst_slot, peer):
        return pltpu.make_async_remote_copy(
            sent.at[kind, src_slot], owned.at[kind, dst_slot],
            send_sem.at[kind, src_slot], recv_sem.at[kind, dst_slot],
            device_id=(g, peer), device_id_type=MESH)

    def copy_back(kind, src_slot, dst_slot, peer):
        return pltpu.make_async_remote_copy(
            stage.at[kind, src_slot], back.at[kind, dst_slot],
            send_sem.at[2 + kind, src_slot], recv_sem.at[2 + kind, dst_slot],
            device_id=(g, peer), device_id_type=MESH)

    def copy_neg(slot, send_slot, peer):
        return pltpu.make_async_remote_copy(
            negs.at[slot], negs.at[slot], gsend_sem.at[0, send_slot], grecv_sem.at[0, slot],
            device_id=(peer, o), device_id_type=MESH)

    def copy_term(src_slot, dst_slot, peer):
        return pltpu.make_async_remote_copy(
            term.at[src_slot], term_in.at[dst_slot], gsend_sem.at[1, src_slot], grecv_sem.at[1, dst_slot],
            device_id=(peer, o), device_id_type=MESH)

    for kind in (0, 1):
        @pl.loop(1, owners)
        def _(k):
            peer = xor(o, owners - k, owners)
            copy_in(kind, peer, o, peer).start()

        owned[kind, pl.ds(o, 1)] = sent[kind, pl.ds(o, 1)]

    def wait_in(kind, step):
        for j in range(step_peers):
            src = step * step_peers + j

            @pl.when(src != o)
            def _():
                copy_in(kind, src, src, src).wait_recv()

    def normalized(kind, step):
        values = owned[kind, pl.ds(step * step_peers, step_peers)].astype(f32).reshape(span, width)
        inv = 1.0 / jnp.sqrt(jnp.sum(values * values, axis=1, keepdims=True) + epsilon)
        return values * inv, inv

    def finish(kind, step, grad, unit, inv):
        inner = jnp.sum(unit * grad, axis=1, keepdims=True)
        grad = ((grad - unit * inner) * inv).reshape(step_peers, c, width).astype(bf16)
        stage[kind, pl.ds(step * step_peers, step_peers)] = grad
        for j in range(step_peers):
            peer = step * step_peers + j

            @pl.when(peer != o)
            def _():
                copy_back(kind, peer, o, peer).start()

            @pl.when(peer == o)
            def _():
                back[kind, pl.ds(peer, 1)] = grad[j:j + 1]

    @pl.loop(0, steps)
    def _(k):
        step = xor(my_step, k, steps)
        wait_in(0, step)
        unit, _ = normalized(0, step)
        keys[pl.ds(pl.multiple_of(step * span, span), span)] = unit.astype(bf16)

    choose = (neg_col[...] == lax.broadcasted_iota(jnp.int32, (n_neg, rows), 1)).astype(f32).astype(bf16)
    negs[pl.ds(g, 1)] = dot(choose, keys[:rows]).astype(bf16).reshape(1, n_neg, width)

    @pl.loop(1, groups)
    def _(k):
        peer = xor(g, k, groups)
        copy_neg(g, peer, peer).start()

    @pl.loop(1, groups)
    def _(k):
        peer = xor(g, k, groups)
        copy_neg(peer, peer, peer).wait_recv()

    keys[rows:] = negs[...].astype(f32).reshape(n_all, width).astype(bf16)

    col = lax.broadcasted_iota(jnp.int32, (span, rows + n_all), 1)
    keep = jnp.logical_or(col < rows, (col - rows) // n_neg != g)
    lane = lax.broadcasted_iota(jnp.int32, (span, rows), 1)
    sub = lax.broadcasted_iota(jnp.int32, (span, rows + n_all), 0)
    sub_l = lax.broadcasted_iota(jnp.int32, (span, rows), 0)

    loss_out[...] = jnp.zeros_like(loss_out)

    @pl.loop(0, steps)
    def _(k):
        step = xor(my_step, k, steps)
        row0 = pl.multiple_of(step * span, span)
        wait_in(1, step)
        unit, inv = normalized(1, step)
        half = unit.astype(bf16)
        qh[pl.ds(row0, span)] = half
        s = dot(half, keys[...], ((1,), (1,))) * logit_scale
        e = jnp.where(keep, jnp.exp(s), 0.0)
        denom = jnp.sum(e, axis=1, keepdims=True)
        own = col == sub + row0
        loss = jnp.log(denom) - jnp.sum(jnp.where(own, s, 0.0), axis=1, keepdims=True)
        loss_out[...] += jnp.sum(jnp.where(lane == sub_l + row0, loss, 0.0), axis=0, keepdims=True)
        weight = e / denom - jnp.where(own, 1.0, 0.0)
        coef[pl.ds(row0, span)] = weight.astype(bf16).astype(f32)
        finish(1, step, dot(weight.astype(bf16), keys[...]) * logit_scale, unit, inv)

    coef_t = jnp.transpose(coef[...])
    term[...] = (dot(coef_t[rows:].astype(bf16), qh[...]) * logit_scale).astype(bf16).reshape(groups, n_neg, width)

    @pl.loop(1, groups)
    def _(k):
        peer = xor(g, k, groups)
        copy_term(peer, g, peer).start()

    term_in[pl.ds(g, 1)] = term[pl.ds(g, 1)]
    dp[...] = dot(coef_t[:rows].astype(bf16), qh[...]) * logit_scale

    @pl.loop(1, groups)
    def _(k):
        peer = xor(g, k, groups)
        copy_term(peer, peer, peer).wait_recv()

    which = lax.broadcasted_iota(jnp.int32, (rows, n_neg), 0)
    place = (neg_row[...] == which).astype(f32)
    place = jnp.concatenate([place] * groups, axis=1).astype(bf16)
    terms = term_in[...].astype(f32).reshape(n_all, width).astype(bf16)
    dp[...] += dot(place, terms)

    @pl.loop(0, steps)
    def _(k):
        step = xor(my_step, steps - 1 - k, steps)
        unit, inv = normalized(0, step)
        finish(0, step, dp[pl.ds(pl.multiple_of(step * span, span), span)], unit, inv)

    unpick = (send_row[...] == lax.broadcasted_iota(jnp.int32, (rows, rows), 0)).astype(f32).astype(bf16)
    for kind, out in ((1, q_out), (0, p_out)):
        @pl.loop(1, owners)
        def _(k):
            peer = xor(o, k, owners)
            copy_back(kind, peer, peer, peer).wait_recv()

        out[...] = dot(unpick, back[kind].astype(f32).reshape(rows, width).astype(bf16)).astype(bf16)

    @pl.loop(1, owners)
    def _(k):
        peer = xor(o, k, owners)
        for kind in (0, 1):
            copy_in(kind, peer, o, peer).wait_send()
            copy_back(kind, peer, o, peer).wait_send()

    @pl.loop(1, groups)
    def _(k):
        peer = xor(g, k, groups)
        copy_neg(g, peer, peer).wait_send()
        copy_term(peer, g, peer).wait_send()


def shards(queries, passages, send_order, neg_rows):
    rows, width = queries.shape
    owners, groups = lax.axis_size("owner"), lax.axis_size("group")
    n_neg = neg_rows.shape[1]
    c = rows // owners
    step_peers = min(owners, max(1, 16 // c))
    n_all = groups * n_neg
    vmem = pl.BlockSpec(memory_space=pltpu.VMEM)
    q, p, loss = pl.pallas_call(
        functools.partial(kernel, owners, groups, step_peers),
        out_shape=(
            jax.ShapeDtypeStruct(queries.shape, bf16),
            jax.ShapeDtypeStruct(passages.shape, bf16),
            jax.ShapeDtypeStruct((1, rows), f32),
        ),
        in_specs=[vmem] * 6,
        out_specs=(vmem,) * 3,
        scratch_shapes=[
            pltpu.VMEM((2, owners, c, width), bf16),
            pltpu.VMEM((2, owners, c, width), bf16),
            pltpu.VMEM((rows + n_all, width), bf16),
            pltpu.VMEM((rows, width), bf16),
            pltpu.VMEM((rows, rows + n_all), f32),
            pltpu.VMEM((rows, width), f32),
            pltpu.VMEM((groups, n_neg, width), bf16),
            pltpu.VMEM((groups, n_neg, width), bf16),
            pltpu.VMEM((groups, n_neg, width), bf16),
            pltpu.VMEM((2, owners, c, width), bf16),
            pltpu.VMEM((2, owners, c, width), bf16),
            pltpu.SemaphoreType.DMA((4, owners)),
            pltpu.SemaphoreType.DMA((4, owners)),
            pltpu.SemaphoreType.DMA((2, groups)),
            pltpu.SemaphoreType.DMA((2, groups)),
        ],
        compiler_params=pltpu.CompilerParams(
            collective_id=0, has_side_effects=True, vmem_limit_bytes=48 * 1024 * 1024
        ),
    )(queries, passages, send_order.reshape(rows, 1), send_order, neg_rows.reshape(n_neg, 1), neg_rows)
    return q, p, loss.reshape(rows)


def solution(mesh):
    placed = P(("group", "owner"), None)
    return jax.shard_map(
        shards,
        mesh=mesh,
        in_specs=(placed,) * 4,
        out_specs=(placed, placed, P(("group", "owner"))),
        check_vma=False,
    )
```

profile of v0, /device:TPU:3, one launch (start us, length us, event | category | flops | bytes accessed | tf_op | source)
XLA Modules:
  0.0 59.4 jit_solution(14902684758346547071)
XLA Ops:
  0.6 0.0 copy-start.3
  0.6 0.6 %copy-done.3 = s32[1,8]{1,0:T(1,128)S(1)} copy-done((s32[1,8]{1,0:T(1,128)S(1)}, s32[1,8]{1,0:T(1,128)}, u32[]{:S(2)}) %copy-start.3) | copy-done | bytes 56
  1.3 0.0 copy-start.2
  1.3 0.1 copy.8.neg_col
  1.4 0.6 copy-done.2
  1.9 0.1 copy.7.send_col
  2.0 0.0 copy-start
  2.0 1.0 %copy-done = bf16[64,4096]{1,0:T(8,128)(2,1)S(1)} copy-done((bf16[64,4096]{1,0:T(8,128)(2,1)S(1)}, bf16[64,4096]{1,0:T(8,128)(2,1)}, u32[]{:S(2)}) %copy-start) | copy-done | bytes 524312
  3.1 0.0 copy-start.1
  3.1 1.0 %copy-done.1 = bf16[64,4096]{1,0:T(8,128)(2,1)S(1)} copy-done((bf16[64,4096]{1,0:T(8,128)(2,1)S(1)}, bf16[64,4096]{1,0:T(8,128)(2,1)}, u32[]{:S(2)}) %copy-start.1) | copy-done | bytes 524312
  4.1 53.2 %shard_map.67 = (bf16[64,4096]{1,0:T(8,128)(2,1)S(1)}, bf16[64,4096]{1,0:T(8,128)(2,1)S(1)}, f32[1,64]{1,0:T(1,128)S(1)}) custom-call(bf16[64,4096]{1,0:T(8,128)(2,1)S(1)} %copy-done, bf16[64,4096]{1,0:T(8,128)(2,1)S(1)} %copy-done.1, s32[64,1]{1,0:T(8,128)S(1)} %copy.7.send_col, s32[1,64]{1,0:T(1,128)S(1)} %copy-done.2, s32[8,1]{1,0:T(8,128)S(1)} %copy.8.neg_col, ...), custom_call_target="tpu_custom_call" | custom-call | tf_op jit(solution)/shard_map/pallas_call | solution.py:224
  57.3 0.8 %copy.12 = bf16[64,4096]{1,0:T(8,128)(2,1)} copy(bf16[64,4096]{1,0:T(8,128)(2,1)S(1)} %get-tuple-element.12) | data formatting | bytes 1048576
  58.1 0.8 %copy.13 = bf16[64,4096]{1,0:T(8,128)(2,1)} copy(bf16[64,4096]{1,0:T(8,128)(2,1)S(1)} %get-tuple-element.13) | data formatting | bytes 1048576
  58.9 0.5 copy.14
Async XLA Ops:
  0.6 0.7 %copy-start.3 = (s32[1,8]{1,0:T(1,128)S(1)}, s32[1,8]{1,0:T(1,128)}, u32[]{:S(2)}) copy-start(s32[1,8]{1,0:T(1,128)} %neg_row.1) | copy-start | bytes 100
  1.3 0.7 %copy-start.2 = (s32[1,64]{1,0:T(1,128)S(1)}, s32[1,64]{1,0:T(1,128)}, u32[]{:S(2)}) copy-start(s32[1,64]{1,0:T(1,128)} %send_row.1) | copy-start | bytes 772
  2.0 1.0 %copy-start = (bf16[64,4096]{1,0:T(8,128)(2,1)S(1)}, bf16[64,4096]{1,0:T(8,128)(2,1)}, u32[]{:S(2)}) copy-start(bf16[64,4096]{1,0:T(8,128)(2,1)} %q_ref.1) | copy-start | bytes 1572868
  3.1 1.0 %copy-start.1 = (bf16[64,4096]{1,0:T(8,128)(2,1)S(1)}, bf16[64,4096]{1,0:T(8,128)(2,1)}, u32[]{:S(2)}) copy-start(bf16[64,4096]{1,0:T(8,128)(2,1)} %p_ref.1) | copy-start | bytes 1572868
where the time goes:
time: 59.6 us; the launch traced here: 59.4 us
  Pallas kernels  53.2 us (89%)
  local copies, waits for them, and re-layouts  5.58 us (9%)
  between operations  0.65 us (1%)
    pallas_call x1, Pallas kernels, shards(): pl.pallas_call(functools.partial(kernel, owners, groups, step_peers), out...  53.2 us
    unnamed x11, local copies, waits for them, and re-layouts  5.4 us

commit v1 on v0

--- a/solution.py
+++ b/solution.py
@@ -25,22 +25,54 @@
     return lax.dot_general(a, b, (dims, ((), ())), preferred_element_type=f32)
 
 
+def unpicked(send_row, values):
+    rows = send_row.shape[1]
+    unpick = (send_row[...] == lax.broadcasted_iota(jnp.int32, (rows, rows), 0)).astype(f32).astype(bf16)
+    return dot(unpick, values.astype(f32).reshape(rows, values.shape[2]).astype(bf16)).astype(bf16)
+
+
+def place_kernel(parts, q_ref, p_back, loss_ref, send_row, q_hbm, p_hbm, loss_hbm, p_out, sems):
+    width = q_ref.shape[1] // parts
+    copies = [
+        pltpu.make_async_copy(q_ref, q_hbm, sems.at[0]),
+        pltpu.make_async_copy(loss_ref, loss_hbm, sems.at[1]),
+    ]
+    for copy in copies:
+        copy.start()
+    for i in range(parts):
+        cols = pl.ds(i * width, width)
+        p_out[:, cols] = unpicked(send_row, p_back[:, :, cols])
+        copies.append(pltpu.make_async_copy(p_out.at[:, cols], p_hbm.at[:, cols], sems.at[2 + i]))
+        copies[-1].start()
+    for copy in copies:
+        copy.wait()
+
+
 def kernel(
     owners, groups, step_peers,
-    q_ref, p_ref, send_col, send_row, neg_col, neg_row,
-    q_out, p_out, loss_out,
-    sent, owned, keys, qh, coef, dp, negs, term, term_in, stage, back,
-    send_sem, recv_sem, gsend_sem, grecv_sem,
+    q_hbm, p_hbm, send_hbm, neg_hbm,
+    q_out, p_back, loss_out,
+    q_ref, p_ref, send_row, neg_row,
+    sent, owned, keys, qh, coef, dp, negs, term, term_in, stage, q_back,
+    load_sem, send_sem, recv_sem, gsend_sem, grecv_sem,
 ):
     rows, width = q_ref.shape
     c = rows // owners
-    n_neg = neg_col.shape[0]
+    n_neg = neg_row.shape[1]
+    back = (p_back, q_back)
     n_all = groups * n_neg
     steps = owners // step_peers
     span = step_peers * c
     g, o = lax.axis_index("group"), lax.axis_index("owner")
     my_step = o // step_peers
 
+    loads = [
+        pltpu.make_async_copy(src, dst, load_sem.at[i])
+        for i, (src, dst) in enumerate(
+            ((send_hbm, send_row), (p_hbm, p_ref), (q_hbm, q_ref), (neg_hbm, neg_row)))
+    ]
+    for load in loads:
+        load.start()
     barrier = pltpu.get_barrier_semaphore()
 
     @pl.loop(1, owners)
@@ -50,11 +82,6 @@
     @pl.loop(1, groups)
     def _(k):
         pl.semaphore_signal(barrier, inc=1, device_id=(xor(g, k, groups), o), device_id_type=MESH)
-
-    pick = (send_col[...] == lax.broadcasted_iota(jnp.int32, (rows, rows), 1)).astype(f32).astype(bf16)
-    sent[0] = dot(pick, p_ref[...]).reshape(owners, c, width).astype(bf16)
-    sent[1] = dot(pick, q_ref[...]).reshape(owners, c, width).astype(bf16)
-    pl.semaphore_wait(barrier, owners + groups - 2)
 
     def copy_in(kind, src_slot, dst_slot, peer):
         return pltpu.make_async_remote_copy(
@@ -64,7 +91,7 @@
 
     def copy_back(kind, src_slot, dst_slot, peer):
         return pltpu.make_async_remote_copy(
-            stage.at[kind, src_slot], back.at[kind, dst_slot],
+            stage.at[kind, src_slot], back[kind].at[dst_slot],
             send_sem.at[2 + kind, src_slot], recv_sem.at[2 + kind, dst_slot],
             device_id=(g, peer), device_id_type=MESH)
 
@@ -78,13 +105,27 @@
             term.at[src_slot], term_in.at[dst_slot], gsend_sem.at[1, src_slot], grecv_sem.at[1, dst_slot],
             device_id=(peer, o), device_id_type=MESH)
 
-    for kind in (0, 1):
+    def column(row_values):
+        n = row_values.shape[1]
+        square = (n, n)
+        diag = lax.broadcasted_iota(jnp.int32, square, 0) == lax.broadcasted_iota(jnp.int32, square, 1)
+        return jnp.sum(jnp.where(diag, row_values.astype(f32), 0.0), axis=1, keepdims=True).astype(jnp.int32)
+
+    loads[0].wait()
+    pick = (column(send_row[...]) == lax.broadcasted_iota(jnp.int32, (rows, rows), 1)).astype(f32).astype(bf16)
+    for kind, source in ((0, p_ref), (1, q_ref)):
+        loads[1 + kind].wait()
+        sent[kind] = dot(pick, source[...]).reshape(owners, c, width).astype(bf16)
+        if kind == 0:
+            pl.semaphore_wait(barrier, owners + groups - 2)
+
         @pl.loop(1, owners)
         def _(k):
-            peer = xor(o, owners - k, owners)
+            peer = xor(o, k, owners)
             copy_in(kind, peer, o, peer).start()
 
         owned[kind, pl.ds(o, 1)] = sent[kind, pl.ds(o, 1)]
+    loads[3].wait()
 
     def wait_in(kind, step):
         for j in range(step_peers):
@@ -112,7 +153,7 @@
 
             @pl.when(peer == o)
             def _():
-                back[kind, pl.ds(peer, 1)] = grad[j:j + 1]
+                back[kind][pl.ds(peer, 1)] = grad[j:j + 1]
 
     @pl.loop(0, steps)
     def _(k):
@@ -121,7 +162,7 @@
         unit, _ = normalized(0, step)
         keys[pl.ds(pl.multiple_of(step * span, span), span)] = unit.astype(bf16)
 
-    choose = (neg_col[...] == lax.broadcasted_iota(jnp.int32, (n_neg, rows), 1)).astype(f32).astype(bf16)
+    choose = (column(neg_row[...]) == lax.broadcasted_iota(jnp.int32, (n_neg, rows), 1)).astype(f32).astype(bf16)
     negs[pl.ds(g, 1)] = dot(choose, keys[:rows]).astype(bf16).reshape(1, n_neg, width)
 
     @pl.loop(1, groups)
@@ -178,26 +219,26 @@
         peer = xor(g, k, groups)
         copy_term(peer, peer, peer).wait_recv()
 
-    which = lax.broadcasted_iota(jnp.int32, (rows, n_neg), 0)
-    place = (neg_row[...] == which).astype(f32)
-    place = jnp.concatenate([place] * groups, axis=1).astype(bf16)
-    terms = term_in[...].astype(f32).reshape(n_all, width).astype(bf16)
-    dp[...] += dot(place, terms)
+    which = lax.broadcasted_iota(jnp.int32, (span, n_neg), 0)
 
     @pl.loop(0, steps)
     def _(k):
-        step = xor(my_step, steps - 1 - k, steps)
+        step = xor(my_step, (k + steps // 2) % steps, steps)
+        row0 = pl.multiple_of(step * span, span)
+        place = (neg_row[...] == which + row0).astype(f32)
+        place = jnp.concatenate([place] * groups, axis=1).astype(bf16)
+        terms = term_in[...].astype(f32).reshape(n_all, width).astype(bf16)
         unit, inv = normalized(0, step)
-        finish(0, step, dp[pl.ds(pl.multiple_of(step * span, span), span)], unit, inv)
-
-    unpick = (send_row[...] == lax.broadcasted_iota(jnp.int32, (rows, rows), 0)).astype(f32).astype(bf16)
-    for kind, out in ((1, q_out), (0, p_out)):
+        finish(0, step, dp[pl.ds(row0, span)] + dot(place, terms), unit, inv)
+
+    for kind in (1, 0):
         @pl.loop(1, owners)
         def _(k):
             peer = xor(o, k, owners)
             copy_back(kind, peer, peer, peer).wait_recv()
 
-        out[...] = dot(unpick, back[kind].astype(f32).reshape(rows, width).astype(bf16)).astype(bf16)
+        if kind == 1:
+            q_out[...] = unpicked(send_row, q_back[...])
 
     @pl.loop(1, owners)
     def _(k):
@@ -221,36 +262,57 @@
     step_peers = min(owners, max(1, 16 // c))
     n_all = groups * n_neg
     vmem = pl.BlockSpec(memory_space=pltpu.VMEM)
-    q, p, loss = pl.pallas_call(
+    hbm = pl.BlockSpec(memory_space=pltpu.HBM)
+    blocks = (owners, c, width)
+    neg_blocks = (groups, n_neg, width)
+    q_placed, p_back, loss = pl.pallas_call(
         functools.partial(kernel, owners, groups, step_peers),
         out_shape=(
             jax.ShapeDtypeStruct(queries.shape, bf16),
-            jax.ShapeDtypeStruct(passages.shape, bf16),
+            jax.ShapeDtypeStruct(blocks, bf16),
             jax.ShapeDtypeStruct((1, rows), f32),
         ),
-        in_specs=[vmem] * 6,
+        in_specs=[hbm] * 4,
         out_specs=(vmem,) * 3,
         scratch_shapes=[
-            pltpu.VMEM((2, owners, c, width), bf16),
-            pltpu.VMEM((2, owners, c, width), bf16),
+            pltpu.VMEM((rows, width), bf16),
+            pltpu.VMEM((rows, width), bf16),
+            pltpu.VMEM((1, rows), jnp.int32),
+            pltpu.VMEM((1, n_neg), jnp.int32),
+            pltpu.VMEM((2,) + blocks, bf16),
+            pltpu.VMEM((2,) + blocks, bf16),
             pltpu.VMEM((rows + n_all, width), bf16),
             pltpu.VMEM((rows, width), bf16),
             pltpu.VMEM((rows, rows + n_all), f32),
             pltpu.VMEM((rows, width), f32),
-            pltpu.VMEM((groups, n_neg, width), bf16),
-            pltpu.VMEM((groups, n_neg, width), bf16),
-            pltpu.VMEM((groups, n_neg, width), bf16),
-            pltpu.VMEM((2, owners, c, width), bf16),
-            pltpu.VMEM((2, owners, c, width), bf16),
+            pltpu.VMEM(neg_blocks, bf16),
+            pltpu.VMEM(neg_blocks, bf16),
+            pltpu.VMEM(neg_blocks, bf16),
+            pltpu.VMEM((2,) + blocks, bf16),
+            pltpu.VMEM(blocks, bf16),
+            pltpu.SemaphoreType.DMA((4,)),
             pltpu.SemaphoreType.DMA((4, owners)),
             pltpu.SemaphoreType.DMA((4, owners)),
             pltpu.SemaphoreType.DMA((2, groups)),
             pltpu.SemaphoreType.DMA((2, groups)),
         ],
         compiler_params=pltpu.CompilerParams(
-            collective_id=0, has_side_effects=True, vmem_limit_bytes=48 * 1024 * 1024
+            collective_id=0, has_side_effects=True, vmem_limit_bytes=67043328
         ),
-    )(queries, passages, send_order.reshape(rows, 1), send_order, neg_rows.reshape(n_neg, 1), neg_rows)
+    )(queries, passages, send_order, neg_rows)
+    parts = 2
+    q, p, loss = pl.pallas_call(
+        functools.partial(place_kernel, parts),
+        out_shape=(
+            jax.ShapeDtypeStruct(queries.shape, bf16),
+            jax.ShapeDtypeStruct(passages.shape, bf16),
+            jax.ShapeDtypeStruct((1, rows), f32),
+        ),
+        in_specs=[vmem] * 4,
+        out_specs=(hbm,) * 3,
+        scratch_shapes=[pltpu.VMEM((rows, width), bf16), pltpu.SemaphoreType.DMA((2 + parts,))],
+        compiler_params=pltpu.CompilerParams(vmem_limit_bytes=8 * 1024 * 1024),
+    )(q_placed, p_back, loss, send_order)
     return q, p, loss.reshape(rows)
 
 

time: 59.6 us -> 57.9 us (0.971)
  the two profiles are of different devices: /device:TPU:3 before, /device:TPU:11 now
where the time goes in v1:
time: 57.9 us; the launch traced here: 57.6 us
  Pallas kernels  54.2 us (94%)
  local copies, waits for them, and re-layouts  2.75 us (5%)
  between operations  0.66 us (1%)
    pallas_call x1, Pallas kernels, shards(): pl.pallas_call(functools.partial(kernel, owners, groups, step_peers), out...  53.2 us
    unnamed x8, local copies, waits for them, and re-layouts  2.75 us

profile of v1, /device:TPU:11, one launch (start us, length us, event | category | flops | bytes accessed | tf_op | source)
XLA Modules:
  0.0 57.6 jit_solution(9099160348412680361)
XLA Ops:
  0.6 53.2 %shard_map.67 = (bf16[64,4096]{1,0:T(8,128)(2,1)}, bf16[8,8,4096]{2,1,0:T(8,128)(2,1)}, f32[1,64]{1,0:T(1,128)}) custom-call(bf16[64,4096]{1,0:T(8,128)(2,1)} %q_hbm.1, bf16[64,4096]{1,0:T(8,128)(2,1)} %p_hbm.1, s32[1,64]{1,0:T(1,128)} %send_row.1, s32[1,8]{1,0:T(1,128)} %neg_hbm.1), custom_call_target="tpu_custom_call" | custom-call | tf_op jit(solution)/shard_map/pallas_call | solution.py:268
  53.8 0.0 copy-start.2
  53.8 0.0 copy-start.3
  53.8 0.6 %copy-done.2 = s32[1,64]{1,0:T(1,128)S(1)} copy-done((s32[1,64]{1,0:T(1,128)S(1)}, s32[1,64]{1,0:T(1,128)}, u32[]{:S(2)}) %copy-start.2) | copy-done | bytes 280
  54.5 0.0 copy-done.3
  54.5 0.0 copy-start
  54.5 1.0 %copy-done = bf16[64,4096]{1,0:T(8,128)(2,1)S(1)} copy-done((bf16[64,4096]{1,0:T(8,128)(2,1)S(1)}, bf16[64,4096]{1,0:T(8,128)(2,1)}, u32[]{:S(2)}) %copy-start) | copy-done | bytes 524312
  55.5 0.0 copy-start.1
  55.5 1.0 %copy-done.1 = bf16[8,8,4096]{2,1,0:T(8,128)(2,1)S(1)} copy-done((bf16[8,8,4096]{2,1,0:T(8,128)(2,1)S(1)}, bf16[8,8,4096]{2,1,0:T(8,128)(2,1)}, u32[]{:S(2)}) %copy-start.1) | copy-done | bytes 524312
  56.6 1.0 %shard_map.68 = (bf16[64,4096]{1,0:T(8,128)(2,1)}, bf16[64,4096]{1,0:T(8,128)(2,1)}, f32[1,64]{1,0:T(1,128)}) custom-call(bf16[64,4096]{1,0:T(8,128)(2,1)S(1)} %copy-done, bf16[8,8,4096]{2,1,0:T(8,128)(2,1)S(1)} %copy-done.1, f32[1,64]{1,0:T(1,128)S(1)} %copy-done.3, s32[1,64]{1,0:T(1,128)S(1)} %copy-done.2), custom_call_target="tpu_custom_call" | custom-call | tf_op jit(solution)/shard_map/pallas_call | solution.py:304
Async XLA Ops:
  53.8 0.7 %copy-start.2 = (s32[1,64]{1,0:T(1,128)S(1)}, s32[1,64]{1,0:T(1,128)}, u32[]{:S(2)}) copy-start(s32[1,64]{1,0:T(1,128)} %send_row.1) | copy-start | bytes 772
  53.8 0.7 %copy-start.3 = (f32[1,64]{1,0:T(1,128)S(1)}, f32[1,64]{1,0:T(1,128)}, u32[]{:S(2)}) copy-start(f32[1,64]{1,0:T(1,128)} %get-tuple-element.11.loss_ref) | copy-start | bytes 772
  54.5 1.0 %copy-start = (bf16[64,4096]{1,0:T(8,128)(2,1)S(1)}, bf16[64,4096]{1,0:T(8,128)(2,1)}, u32[]{:S(2)}) copy-start(bf16[64,4096]{1,0:T(8,128)(2,1)} %get-tuple-element.9.q_ref) | copy-start | bytes 1572868
  55.5 1.0 %copy-start.1 = (bf16[8,8,4096]{2,1,0:T(8,128)(2,1)S(1)}, bf16[8,8,4096]{2,1,0:T(8,128)(2,1)}, u32[]{:S(2)}) copy-start(bf16[8,8,4096]{2,1,0:T(8,128)(2,1)} %get-tuple-element.10.p_back) | copy-start | bytes 1572868

commit v2 on v1

--- a/solution.py
+++ b/solution.py
@@ -31,28 +31,33 @@
     return dot(unpick, values.astype(f32).reshape(rows, values.shape[2]).astype(bf16)).astype(bf16)
 
 
-def place_kernel(parts, q_ref, p_back, loss_ref, send_row, q_hbm, p_hbm, loss_hbm, p_out, sems):
+def place_kernel(parts, q_in, p_in, loss_in, send_in, q_out, p_out, loss_out, q_ref, p_ref, loss_ref, send_row, p_placed, sems):
     width = q_ref.shape[1] // parts
-    copies = [
-        pltpu.make_async_copy(q_ref, q_hbm, sems.at[0]),
-        pltpu.make_async_copy(loss_ref, loss_hbm, sems.at[1]),
-    ]
-    for copy in copies:
-        copy.start()
-    for i in range(parts):
-        cols = pl.ds(i * width, width)
-        p_out[:, cols] = unpicked(send_row, p_back[:, :, cols])
-        copies.append(pltpu.make_async_copy(p_out.at[:, cols], p_hbm.at[:, cols], sems.at[2 + i]))
-        copies[-1].start()
-    for copy in copies:
-        copy.wait()
+    spans = [pl.ds(i * width, width) for i in range(parts)]
+    pairs = [(send_in, send_row)] + [(p_in.at[:, :, cols], p_ref.at[:, :, cols]) for cols in spans]
+    pairs += [(q_in, q_ref), (loss_in, loss_ref)]
+    loads = [pltpu.make_async_copy(src, dst, sems.at[0, i]) for i, (src, dst) in enumerate(pairs)]
+    pairs = [(p_placed.at[:, cols], p_out.at[:, cols]) for cols in spans] + [(q_ref, q_out), (loss_ref, loss_out)]
+    stores = [pltpu.make_async_copy(src, dst, sems.at[1, i]) for i, (src, dst) in enumerate(pairs)]
+    for load in loads:
+        load.start()
+    loads[0].wait()
+    for i, cols in enumerate(spans):
+        loads[1 + i].wait()
+        p_placed[:, cols] = unpicked(send_row, p_ref[:, :, cols])
+        stores[i].start()
+    for i in (parts, parts + 1):
+        loads[1 + i].wait()
+        stores[i].start()
+    for store in stores:
+        store.wait()
 
 
 def kernel(
     owners, groups, step_peers,
     q_hbm, p_hbm, send_hbm, neg_hbm,
-    q_out, p_back, loss_out,
-    q_ref, p_ref, send_row, neg_row,
+    q_out, p_back, loss_hbm,
+    q_ref, p_ref, send_row, neg_row, q_placed, loss_out,
     sent, owned, keys, qh, coef, dp, negs, term, term_in, stage, q_back,
     load_sem, send_sem, recv_sem, gsend_sem, grecv_sem,
 ):
@@ -127,6 +132,10 @@
         owned[kind, pl.ds(o, 1)] = sent[kind, pl.ds(o, 1)]
     loads[3].wait()
 
+    keep_own = pltpu.make_async_copy(stage.at[0, o], p_back.at[o], load_sem.at[4])
+    put_q = pltpu.make_async_copy(q_placed, q_out, load_sem.at[5])
+    put_loss = pltpu.make_async_copy(loss_out, loss_hbm, load_sem.at[6])
+
     def wait_in(kind, step):
         for j in range(step_peers):
             src = step * step_peers + j
@@ -153,7 +162,10 @@
 
             @pl.when(peer == o)
             def _():
-                back[kind][pl.ds(peer, 1)] = grad[j:j + 1]
+                if kind == 0:
+                    keep_own.start()
+                else:
+                    q_back[pl.ds(peer, 1)] = grad[j:j + 1]
 
     @pl.loop(0, steps)
     def _(k):
@@ -187,7 +199,8 @@
 
     @pl.loop(0, steps)
     def _(k):
-        step = xor(my_step, k, steps)
+        half_way, later = steps // 2, (k + steps - 1) // steps
+        step = xor(my_step, half_way * (1 - later) + k - later * (1 - k // (half_way + 1)), steps)
         row0 = pl.multiple_of(step * span, span)
         wait_in(1, step)
         unit, inv = normalized(1, step)
@@ -203,6 +216,7 @@
         coef[pl.ds(row0, span)] = weight.astype(bf16).astype(f32)
         finish(1, step, dot(weight.astype(bf16), keys[...]) * logit_scale, unit, inv)
 
+    put_loss.start()
     coef_t = jnp.transpose(coef[...])
     term[...] = (dot(coef_t[rows:].astype(bf16), qh[...]) * logit_scale).astype(bf16).reshape(groups, n_neg, width)
 
@@ -238,7 +252,8 @@
             copy_back(kind, peer, peer, peer).wait_recv()
 
         if kind == 1:
-            q_out[...] = unpicked(send_row, q_back[...])
+            q_placed[...] = unpicked(send_row, q_back[...])
+            put_q.start()
 
     @pl.loop(1, owners)
     def _(k):
@@ -252,6 +267,9 @@
         peer = xor(g, k, groups)
         copy_neg(g, peer, peer).wait_send()
         copy_term(peer, g, peer).wait_send()
+
+    for copy in (keep_own, put_q, put_loss):
+        copy.wait()
 
 
 def shards(queries, passages, send_order, neg_rows):
@@ -261,7 +279,6 @@
     c = rows // owners
     step_peers = min(owners, max(1, 16 // c))
     n_all = groups * n_neg
-    vmem = pl.BlockSpec(memory_space=pltpu.VMEM)
     hbm = pl.BlockSpec(memory_space=pltpu.HBM)
     blocks = (owners, c, width)
     neg_blocks = (groups, n_neg, width)
@@ -273,12 +290,14 @@
             jax.ShapeDtypeStruct((1, rows), f32),
         ),
         in_specs=[hbm] * 4,
-        out_specs=(vmem,) * 3,
+        out_specs=(hbm,) * 3,
         scratch_shapes=[
             pltpu.VMEM((rows, width), bf16),
             pltpu.VMEM((rows, width), bf16),
             pltpu.VMEM((1, rows), jnp.int32),
             pltpu.VMEM((1, n_neg), jnp.int32),
+            pltpu.VMEM((rows, width), bf16),
+            pltpu.VMEM((1, rows), f32),
             pltpu.VMEM((2,) + blocks, bf16),
             pltpu.VMEM((2,) + blocks, bf16),
             pltpu.VMEM((rows + n_all, width), bf16),
@@ -290,7 +309,7 @@
             pltpu.VMEM(neg_blocks, bf16),
             pltpu.VMEM((2,) + blocks, bf16),
             pltpu.VMEM(blocks, bf16),
-            pltpu.SemaphoreType.DMA((4,)),
+            pltpu.SemaphoreType.DMA((7,)),
             pltpu.SemaphoreType.DMA((4, owners)),
             pltpu.SemaphoreType.DMA((4, owners)),
             pltpu.SemaphoreType.DMA((2, groups)),
@@ -308,10 +327,17 @@
             jax.ShapeDtypeStruct(passages.shape, bf16),
             jax.ShapeDtypeStruct((1, rows), f32),
         ),
-        in_specs=[vmem] * 4,
+        in_specs=[hbm] * 4,
         out_specs=(hbm,) * 3,
-        scratch_shapes=[pltpu.VMEM((rows, width), bf16), pltpu.SemaphoreType.DMA((2 + parts,))],
-        compiler_params=pltpu.CompilerParams(vmem_limit_bytes=8 * 1024 * 1024),
+        scratch_shapes=[
+            pltpu.VMEM((rows, width), bf16),
+            pltpu.VMEM(blocks, bf16),
+            pltpu.VMEM((1, rows), f32),
+            pltpu.VMEM((1, rows), jnp.int32),
+            pltpu.VMEM((rows, width), bf16),
+            pltpu.SemaphoreType.DMA((2, 3 + parts)),
+        ],
+        compiler_params=pltpu.CompilerParams(vmem_limit_bytes=67043328),
     )(q_placed, p_back, loss, send_order)
     return q, p, loss.reshape(rows)
 

time: 57.9 us -> 56.4 us (0.974)
  local copies, waits for them, and re-layouts: 2.75 us -> 0 us
  Pallas kernels: 54.2 us -> 55.6 us
    unnamed x8 -> x0, local copies, waits for them, and re-layouts: 2.75 us -> none
    pallas_call x1, Pallas kernels: 1.04 us -> 2.36 us  [shards(): pl.pallas_call(functools.partial(place_kernel, parts), out_shape=(jax.Sha...]
where the time goes in v2:
time: 56.4 us; the launch traced here: 56.2 us
  Pallas kernels  55.6 us (99%)
  between operations  0.64 us (1%)
    pallas_call x1, Pallas kernels, shards(): pl.pallas_call(functools.partial(kernel, owners, groups, step_peers), out...  53.2 us
    pallas_call x1, Pallas kernels, shards(): pl.pallas_call(functools.partial(place_kernel, parts), out_shape=(jax.Sha...  2.36 us

profile of v2, /device:TPU:11, one launch (start us, length us, event | category | flops | bytes accessed | tf_op | source)
XLA Modules:
  0.0 56.2 jit_solution(8008269967029038924)
XLA Ops:
  0.6 53.2 %shard_map.67 = (bf16[64,4096]{1,0:T(8,128)(2,1)}, bf16[8,8,4096]{2,1,0:T(8,128)(2,1)}, f32[1,64]{1,0:T(1,128)}) custom-call(bf16[64,4096]{1,0:T(8,128)(2,1)} %q_hbm.1, bf16[64,4096]{1,0:T(8,128)(2,1)} %p_hbm.1, s32[1,64]{1,0:T(1,128)} %send_in.1, s32[1,8]{1,0:T(1,128)} %neg_hbm.1), custom_call_target="tpu_custom_call" | custom-call | tf_op jit(solution)/shard_map/pallas_call | solution.py:285
  53.9 2.4 %shard_map.68 = (bf16[64,4096]{1,0:T(8,128)(2,1)}, bf16[64,4096]{1,0:T(8,128)(2,1)}, f32[1,64]{1,0:T(1,128)}) custom-call(bf16[64,4096]{1,0:T(8,128)(2,1)} %get-tuple-element.9.q_in, bf16[8,8,4096]{2,1,0:T(8,128)(2,1)} %get-tuple-element.10.p_in, f32[1,64]{1,0:T(1,128)} %get-tuple-element.11.loss_in, s32[1,64]{1,0:T(1,128)} %send_in.1), custom_call_target="tpu_custom_call" | custom-call | tf_op jit(solution)/shard_map/pallas_call | solution.py:323

commit v3 on v2

--- a/solution.py
+++ b/solution.py
@@ -126,7 +126,7 @@
 
         @pl.loop(1, owners)
         def _(k):
-            peer = xor(o, k, owners)
+            peer = xor(o, owners - k, owners)
             copy_in(kind, peer, o, peer).start()
 
         owned[kind, pl.ds(o, 1)] = sent[kind, pl.ds(o, 1)]
@@ -199,8 +199,7 @@
 
     @pl.loop(0, steps)
     def _(k):
-        half_way, later = steps // 2, (k + steps - 1) // steps
-        step = xor(my_step, half_way * (1 - later) + k - later * (1 - k // (half_way + 1)), steps)
+        step = xor(my_step, k, steps)
         row0 = pl.multiple_of(step * span, span)
         wait_in(1, step)
         unit, inv = normalized(1, step)

time: 56.4 us -> 55.2 us (0.979)
  Pallas kernels: 55.6 us -> 54.3 us
    pallas_call x1, Pallas kernels: 53.2 us -> 52 us  [shards(): pl.pallas_call(functools.partial(kernel, owners, groups, step_peers), out...]
where the time goes in v3:
time: 55.2 us; the launch traced here: 55 us
  Pallas kernels  54.3 us (98%)
  between operations  0.64 us (1%)
    pallas_call x1, Pallas kernels, shards(): pl.pallas_call(functools.partial(kernel, owners, groups, step_peers), out...  52 us
    pallas_call x1, Pallas kernels, shards(): pl.pallas_call(functools.partial(place_kernel, parts), out_shape=(jax.Sha...  2.35 us

profile of v3, /device:TPU:11, one launch (start us, length us, event | category | flops | bytes accessed | tf_op | source)
XLA Modules:
  0.0 55.0 jit_solution(13413200481964986212)
XLA Ops:
  0.6 52.0 %shard_map.67 = (bf16[64,4096]{1,0:T(8,128)(2,1)}, bf16[8,8,4096]{2,1,0:T(8,128)(2,1)}, f32[1,64]{1,0:T(1,128)}) custom-call(bf16[64,4096]{1,0:T(8,128)(2,1)} %q_hbm.1, bf16[64,4096]{1,0:T(8,128)(2,1)} %p_hbm.1, s32[1,64]{1,0:T(1,128)} %send_in.1, s32[1,8]{1,0:T(1,128)} %neg_hbm.1), custom_call_target="tpu_custom_call" | custom-call | tf_op jit(solution)/shard_map/pallas_call | solution.py:284
  52.6 2.4 %shard_map.68 = (bf16[64,4096]{1,0:T(8,128)(2,1)}, bf16[64,4096]{1,0:T(8,128)(2,1)}, f32[1,64]{1,0:T(1,128)}) custom-call(bf16[64,4096]{1,0:T(8,128)(2,1)} %get-tuple-element.9.q_in, bf16[8,8,4096]{2,1,0:T(8,128)(2,1)} %get-tuple-element.10.p_in, f32[1,64]{1,0:T(1,128)} %get-tuple-element.11.loss_in, s32[1,64]{1,0:T(1,128)} %send_in.1), custom_call_target="tpu_custom_call" | custom-call | tf_op jit(solution)/shard_map/pallas_call | solution.py:322
